TPU v7x, 32 devices: a whole 2x2x4 slice. The times are simulated.
32 devices in a mesh: seq: 4 (over y, x), head: 4 (over z), rep: 2 (over core).
Axes of the slice: x: 2, y: 2, z: 4, core: 2. Of those that a mesh axis runs over, the one named last changes fastest.
Arguments:
- query_heads: bfloat16 [2, 8192, 4096], P('rep', 'seq', 'head'), may hold values from -0.59765625 to 0.59765625
- key_heads: bfloat16 [2, 8192, 4096], P('rep', 'seq', 'head'), may hold values from -0.59765625 to 0.59765625
- value_heads: bfloat16 [2, 8192, 4096], P('rep', 'seq', 'head'), may hold values from -6 to 6
- out_cotangent: bfloat16 [2, 8192, 4096], P('rep', 'seq', 'head'), may hold values from -0.19921875 to 0.19921875
- out_weight: bfloat16 [4096, 4096], P('head'), may hold values from -0.09375 to 0.09375
- doc_ends: int32 [2, 7], P('rep'), may hold values from 1 to 8192, as said below
Outputs:
- grad_query: bfloat16 [2, 8192, 4096], P('rep', 'seq', 'head')
- grad_key: bfloat16 [2, 8192, 4096], P('rep', 'seq', 'head')
- grad_value: bfloat16 [2, 8192, 4096], P('rep', 'seq', 'head')
- grad_weight: float32 [4096, 4096], P('head', ('seq', 'rep'))
Inputs may be any that keep to these rules, and one draw needn't show every extreme that they name: `doc_ends`: each row holds 7 strictly increasing document end offsets; its last entry is 8192.
All inputs are finite; a program needn't handle non-finite values.
Results may differ from a plain program's by a relative error of at most 0.0052.
Values may be sent and summed in bfloat16 or wider, within the bound.
No kernel may reach another device: no remote copies, remote signals or barrier semaphores. Data moves between devices by JAX's collectives and lax.ppermute only.
A program may use at most 320 MiB of HBM per device.

v0:
```python
import jax
import jax.numpy as jnp
from jax import lax
from jax.sharding import PartitionSpec as P

HD = 128
BLOCK = 512
highest = lax.Precision.HIGHEST


def prefix(shard, axis, combine, identity, reverse):
    count, here = (lax.axis_size(axis), lax.axis_index(axis))
    everything = jax.tree.map(lambda part: lax.all_gather(part, axis), shard)
    start = jax.tree.map(
        lambda part, zero: jnp.broadcast_to(jnp.asarray(zero, part.dtype), part.shape),
        shard,
        identity,
    )

    def step(k, before):
        at = count - 1 - k if reverse else k
        reached = at > here if reverse else at < here
        new = combine(before, jax.tree.map(lambda part: part[at], everything))
        return jax.tree.map(lambda a, b: jnp.where(reached, a, b), new, before)

    return lax.fori_loop(0, count, step, start)


def doc_counts(positions, ends_row):
    return jnp.sum((ends_row[None, :] <= positions[:, None]).astype(jnp.int32), axis=1)


def local_pass(queries, keys, values, grads, counts, count_before):
    length, heads, width = queries.shape
    blocks = length // BLOCK
    query_blocks = queries.reshape(blocks, BLOCK, heads, width)
    key_blocks = keys.reshape(blocks, BLOCK, heads, width)
    value_blocks = values.reshape(blocks, BLOCK, heads, width)
    grad_blocks = grads.reshape(blocks, BLOCK, heads, width)
    count_blocks = counts.reshape(blocks, BLOCK)
    before_each = jnp.concatenate([jnp.reshape(count_before, (1,)), count_blocks[:-1, -1]])
    last_each = count_blocks[:, -1]
    rows = lax.broadcasted_iota(jnp.int32, (BLOCK, BLOCK), 0)
    cols = lax.broadcasted_iota(jnp.int32, (BLOCK, BLOCK), 1)
    allowed = (
        (count_blocks[:, :, None] == count_blocks[:, None, :]) & (rows >= cols)[None]
    ).astype(jnp.float32)
    scores = jnp.einsum(
        "nthe,nshe->nhts", query_blocks, key_blocks, preferred_element_type=jnp.float32
    )
    attn = (scores * allowed[:, None]).astype(jnp.bfloat16)
    back = jnp.einsum(
        "nthe,nshe->nhts", grad_blocks, value_blocks, preferred_element_type=jnp.float32
    )
    pgrad = (back * allowed[:, None]).astype(jnp.bfloat16)
    out_intra = jnp.einsum(
        "nhts,nshe->nthe", attn, value_blocks, preferred_element_type=jnp.float32
    )
    dq_intra = jnp.einsum("nhts,nshe->nthe", pgrad, key_blocks, preferred_element_type=jnp.float32)
    dk_intra = jnp.einsum(
        "nhts,nthe->nshe", pgrad, query_blocks, preferred_element_type=jnp.float32
    )
    dv_intra = jnp.einsum("nhts,nthe->nshe", attn, grad_blocks, preferred_element_type=jnp.float32)
    first_match = (count_blocks == before_each[:, None])[:, :, None, None]
    last_match = (count_blocks == last_each[:, None])[:, :, None, None]
    keep = (last_each == before_each).astype(jnp.float32)
    tails = jnp.einsum(
        "nshe,nshf->nhef",
        key_blocks * last_match.astype(jnp.bfloat16),
        value_blocks,
        preferred_element_type=jnp.float32,
    )
    head_sums = jnp.einsum(
        "nthe,nthf->nhef",
        query_blocks * first_match.astype(jnp.bfloat16),
        grad_blocks,
        preferred_element_type=jnp.float32,
    )

    def link_step(state, item):
        return (item[0] + item[1] * state, state)

    empty = jnp.zeros((heads, width, width), jnp.float32)
    final_tail, states_before = lax.scan(link_step, empty, (tails, keep))
    final_head, states_after = lax.scan(link_step, empty, (head_sums, keep), reverse=True)
    first_weight = first_match.astype(jnp.float32)
    last_weight = last_match.astype(jnp.float32)
    outputs = out_intra + first_weight * jnp.einsum(
        "nthe,nhef->nthf", query_blocks.astype(jnp.float32), states_before, precision=highest
    )
    dq = dq_intra + first_weight * jnp.einsum(
        "nthf,nhef->nthe", grad_blocks.astype(jnp.float32), states_before, precision=highest
    )
    dk = dk_intra + last_weight * jnp.einsum(
        "nshf,nhef->nshe", value_blocks.astype(jnp.float32), states_after, precision=highest
    )
    dv = dv_intra + last_weight * jnp.einsum(
        "nshe,nhef->nshf", key_blocks.astype(jnp.float32), states_after, precision=highest
    )
    shape = (length, heads, width)
    return (
        outputs.reshape(shape),
        dq.reshape(shape),
        dk.reshape(shape),
        dv.reshape(shape),
        final_tail,
        final_head,
    )


def link_states(earlier, later):
    return (jnp.maximum(earlier[0], later[0]), later[1] + (1.0 - later[0]) * earlier[1])


def on_device(query_heads, key_heads, value_heads, out_cotangent, out_weight, doc_ends):
    length = query_heads.shape[1]
    heads = query_heads.shape[2] // HD
    queries = query_heads[0].reshape(length, heads, HD)
    keys = key_heads[0].reshape(length, heads, HD)
    values = value_heads[0].reshape(length, heads, HD)
    full_cotangent = lax.all_gather(out_cotangent, "head", axis=2, tiled=True)[0]
    grads_flat = lax.dot_general(
        full_cotangent, out_weight, (((1,), (1,)), ((), ())), preferred_element_type=jnp.float32
    ).astype(jnp.bfloat16)
    grads = grads_flat.reshape(length, heads, HD)
    offset = lax.axis_index("seq") * length
    positions = offset + jnp.arange(length, dtype=jnp.int32)
    ends_row = doc_ends[0]
    counts = doc_counts(positions, ends_row)
    count_before = doc_counts(jnp.reshape(offset - 1, (1,)), ends_row)[0]
    outputs, dq, dk, dv, tail, head = local_pass(queries, keys, values, grads, counts, count_before)
    flag = (counts[-1] != count_before).astype(jnp.float32)
    identity = (jnp.zeros((), jnp.float32), jnp.zeros_like(tail))
    flag_before, carry_before = prefix((flag, tail), "seq", link_states, identity, False)
    flag_after, carry_after = prefix((flag, head), "seq", link_states, identity, True)
    entry_weight = (counts == count_before).astype(jnp.float32)[:, None, None]
    exit_weight = (counts == counts[-1]).astype(jnp.float32)[:, None, None]
    outputs = outputs + entry_weight * jnp.einsum(
        "the,hef->thf", queries.astype(jnp.float32), carry_before, precision=highest
    )
    dq = dq + entry_weight * jnp.einsum(
        "thf,hef->the", grads.astype(jnp.float32), carry_before, precision=highest
    )
    dk = dk + exit_weight * jnp.einsum(
        "thf,hef->the", values.astype(jnp.float32), carry_after, precision=highest
    )
    dv = dv + exit_weight * jnp.einsum(
        "the,hef->thf", keys.astype(jnp.float32), carry_after, precision=highest
    )
    flat = heads * HD
    attention_out = outputs.reshape(length, flat).astype(jnp.bfloat16)
    grad_query = dq.reshape(1, length, flat).astype(jnp.bfloat16)
    grad_key = dk.reshape(1, length, flat).astype(jnp.bfloat16)
    grad_value = dv.reshape(1, length, flat).astype(jnp.bfloat16)
    partial_grad = lax.dot_general(
        attention_out, full_cotangent, (((0,), (0,)), ((), ())), preferred_element_type=jnp.float32
    )
    summed = lax.psum(partial_grad, ("seq", "rep"))
    columns = summed.shape[1] // lax.axis_size(("seq", "rep"))
    grad_weight = lax.dynamic_slice_in_dim(
        summed, lax.axis_index(("seq", "rep")) * columns, columns, 1
    )
    return (grad_query, grad_key, grad_value, grad_weight)


def solution(mesh):
    in_specs = (
        P("rep", "seq", "head"),
        P("rep", "seq", "head"),
        P("rep", "seq", "head"),
        P("rep", "seq", "head"),
        P("head", None),
        P("rep", None),
    )
    out_specs = (
        P("rep", "seq", "head"),
        P("rep", "seq", "head"),
        P("rep", "seq", "head"),
        P("head", ("seq", "rep")),
    )
    return jax.shard_map(
        on_device, mesh=mesh, in_specs=in_specs, out_specs=out_specs, check_vma=False
    )
```

profile of v0, /device:TPU:0, one launch (start us, length us, event | category | flops | bytes accessed | tf_op | source)
XLA Modules:
  0.0 711.5 jit_solution(5314023280602779764)
XLA Ops:
  33.0 10.0 %while.60 = (s32[]{:T(128)}, f32[8,128,128]{2,1,0:T(8,128)S(1)}, f32[4,8,128,128]{3,2,1,0:T(8,128)S(1)}, f32[4,8,128,128]{3,2,1,0:T(8,128)}, f32[4]{0:T(128)S(1)}, /*index=5*/s32[]{:T(128)}, s32[]{:T(128)}) while((s32[]{:T(128)}, f32[8,128,128]{2,1,0:T(8,128)S(1)}, f32[4,8,128,128]{3,2,1,0:T(8,128)S(1)}, ...), condition=%wide.region_3.4_spmd.clone, body=%wide.region_2.3_spmd.clone.sunk | while | flops 524291 | bytes 2621560 | solution.py:84
  48.1 11.7 %all-reduce = f32[4]{0:T(128)S(1)} all-reduce(f32[4]{0:T(128)S(1)} %dynamic-update-slice), channel_id=1, replica_groups=mesh['seq'=4,'head'=4,'rep'=2] {'seq'}, use_global_device_ids=true, to_apply=%add | all-reduce | flops 4 | bytes 32
  75.2 11.6 %multiply_convert_fusion = bf16[4,8,512,512]{3,2,1,0:T(8,128)(2,1)} fusion(f32[4,512,512]{2,1,0:T(8,128)} %and_convert_fusion, bf16[4,512,8,128]{1,3,2,0:T(8,128)(2,1)} %copy.184, bf16[4,512,8,128]{1,3,2,0:T(8,128)(2,1)} %copy.175), kind=kOutput, calls=%fused_computation.8 | convolution fusion | flops 2164260864 | bytes 29360128 | tf_op jit(solution)/shard_map/nthe,nshe->nhts/dot_general | solution.py:48
  86.8 17.2 %fusion.24 = f32[4,8,512,128]{3,2,1,0:T(8,128)} fusion(bf16[4,8,512,512]{3,2,1,0:T(8,128)(2,1)} %multiply_convert_fusion, bf16[4,512,8,128]{3,2,1,0:T(8,128)(2,1)} %bitcast.138), kind=kOutput, calls=%fused_computation.39 | convolution fusion | flops 2147483648 | bytes 29360128 | tf_op jit(solution)/shard_map/nhts,nshe->nthe/dot_general | solution.py:56
  104.0 8.4 %bitcast_add_fusion.5 = f32[4,512,8,128]{3,1,2,0:T(8,128)S(1)} fusion(f32[4,8,512,128]{3,2,1,0:T(8,128)} %fusion.24, f32[4,512]{1,0:T(4,128)S(1)} %convert_element_type.133, f32[4,8,128,128]{3,2,1,0:T(8,128)S(1)} %copy-done.4, bf16[4,512,8,128]{1,3,2,0:T(8,128)(2,1)} %copy.184), kind=kOutput, calls=%fused_computation.16 | convolution fusion | flops 3225419776 | bytes 23076864 | tf_op jit(solution)/shard_map/nthe,nhef->nthf/dot_general | solution.py:88
  112.4 8.1 %copy.206 = f32[4,512,8,128]{3,2,1,0:T(8,128)} copy(f32[4,512,8,128]{3,1,2,0:T(8,128)S(1)} %bitcast_add_fusion.5) | data formatting | bytes 16777216 | tf_op jit(solution)/shard_map/add | solution.py:88
  120.5 9.4 %copy.209 = f32[2048,8,128]{0,2,1:T(8,128)} copy(f32[2048,8,128]{2,1,0:T(8,128)} %bitcast.146) | data formatting | bytes 16777216 | tf_op jit(solution)/shard_map/reshape | solution.py:102
  131.8 11.0 %while.61 = (s32[]{:T(128)}, f32[8,128,128]{2,1,0:T(8,128)S(1)}, s32[]{:T(128)}, f32[4,8,128,128]{3,2,1,0:T(8,128)}, f32[4]{0:T(128)S(1)}, /*index=5*/s32[]{:T(128)}, f32[1]{0:T(128)}, s32[]{:T(128)}) while((s32[]{:T(128)}, f32[8,128,128]{2,1,0:T(8,128)S(1)}, s32[]{:T(128)}, f32[4,8,128,128]{3,2,1,0:T(8,128)}, f32[4]{0:T(128)S(1)}, ...), condition=%wide.region_5.6_spmd.clone, body=%wide.region_4.5_spmd.clone.sunk | while | flops 524293 | bytes 1573009 | solution.py:26
  142.8 10.8 %fusion.6 = bf16[2048,8,128]{0,2,1:T(8,128)(2,1)} fusion(f32[2048,8,128]{0,2,1:T(8,128)} %copy.209, f32[8,128,128]{2,1,0:T(8,128)S(1)} %get-tuple-element.364, bf16[2048,8,128]{2,1,0:T(8,128)(2,1)} %bitcast.145, f32[2048]{0:T(1024)S(1)} %get-tuple-element.507), kind=kOutput, calls=%fused_computation.15 | convolution fusion | flops 3227516928 | bytes 17309696 | tf_op jit(solution)/shard_map/the,hef->thf/dot_general | solution.py:138
  153.6 216.7 %all-gather.6.cloned.1.call-done = bf16[1,2048,4096]{2,1,0:T(8,128)(2,1)} async-done(((bf16[1,2048,1024]{2,1,0:T(8,128)(2,1)}), bf16[1,2048,4096]{2,1,0:T(8,128)(2,1)}) %all-gather.6.cloned.1.call-update) | async-done | bytes 16777232 | tf_op jit(solution)/shard_map/all_gather | solution.py:121
  370.3 24.1 %fusion.17 = bf16[2048,1024]{0,1:T(8,128)(2,1)} fusion(bf16[1024,4096]{1,0:T(8,128)(2,1)} %param.18, bf16[1,2048,4096]{2,1,0:T(8,128)(2,1)} %all-gather.6.cloned.1.call-done), kind=kOutput, calls=%fused_computation.34 | convolution fusion | flops 17181966336 | bytes 29360128 | tf_op jit(solution)/shard_map/dot_general | solution.py:122
  394.4 7.8 %reshape_reshape.3 = bf16[4,512,8,128]{1,0,3,2:T(4,128)(2,1)} reshape(bf16[2048,1024]{0,1:T(8,128)(2,1)} %fusion.17) | data formatting | bytes 8388608 | tf_op jit(solution)/shard_map/reshape;reshape | solution.py:39
  402.2 11.6 %multiply_convert_fusion.1 = bf16[4,8,512,512]{3,2,1,0:T(8,128)(2,1)} fusion(f32[4,512,512]{2,1,0:T(8,128)} %and_convert_fusion, bf16[4,512,8,128]{1,0,3,2:T(4,128)(2,1)} %reshape_reshape.3, bf16[4,512,8,128]{3,2,1,0:T(8,128)(2,1)} %bitcast.139), kind=kOutput, calls=%fused_computation.9 | convolution fusion | flops 2164260864 | bytes 29360128 | tf_op jit(solution)/shard_map/nthe,nshe->nhts/dot_general | solution.py:52
  413.9 14.7 %fusion.34 = f32[4,8,512,128]{3,2,1,0:T(8,128)} fusion(bf16[4,8,512,512]{3,2,1,0:T(8,128)(2,1)} %multiply_convert_fusion.1, bf16[4,512,8,128]{1,3,2,0:T(8,128)(2,1)} %copy.175), kind=kOutput, calls=%fused_computation.62 | convolution fusion | flops 2147483648 | bytes 29360128 | tf_op jit(solution)/shard_map/nhts,nshe->nthe/dot_general | solution.py:59
  435.3 10.6 %while.62 = (s32[]{:T(128)}, f32[8,128,128]{2,1,0:T(8,128)S(1)}, f32[4,8,128,128]{3,2,1,0:T(8,128)S(1)}, f32[4,8,128,128]{3,2,1,0:T(8,128)}, f32[4]{0:T(128)S(1)}, /*index=5*/s32[]{:T(128)}, s32[]{:T(128)}, s32[]{:T(128)}) while((s32[]{:T(128)}, f32[8,128,128]{2,1,0:T(8,128)S(1)}, f32[4,8,128,128]{3,2,1,0:T(8,128)S(1)}, ...), condition=%wide.region_7.8_spmd.clone, body=%wide.region_6.7_spmd.clone.sunk | while | flops 524292 | bytes 2621580 | solution.py:85
  446.8 23.6 %fusion.2 = f32[1024,4096]{1,0:T(8,128)} fusion(bf16[2048,1024]{0,1:T(8,128)(2,1)} %bitcast.157, bf16[1,2048,4096]{2,1,0:T(8,128)(2,1)} %all-gather.6.cloned.1.call-done), kind=kOutput, calls=%fused_computation.10 | convolution fusion | flops 17179869184 | bytes 37748736 | tf_op jit(solution)/shard_map/dot_general | solution.py:155
  470.4 9.9 %bitcast_add_fusion.10 = f32[4,512,8,128]{3,1,2,0:T(8,128)S(1)} fusion(f32[4,8,512,128]{3,2,1,0:T(8,128)} %fusion.34, f32[4,512]{1,0:T(4,128)S(1)} %convert_element_type.133, f32[4,8,128,128]{3,2,1,0:T(8,128)} %copy-done.3, bf16[4,512,8,128]{1,0,3,2:T(4,128)(2,1)} %reshape_reshape.3), kind=kOutput, calls=%fused_computation.24 | convolution fusion | flops 3225419776 | bytes 23076864 | tf_op jit(solution)/shard_map/nthf,nhef->nthe/dot_general | solution.py:91
  480.3 8.1 %copy.179 = f32[4,512,8,128]{3,2,1,0:T(8,128)} copy(f32[4,512,8,128]{3,1,2,0:T(8,128)S(1)} %bitcast_add_fusion.10) | data formatting | bytes 16777216 | tf_op jit(solution)/shard_map/add | solution.py:91
  488.4 9.9 %copy.181 = f32[2048,8,128]{0,2,1:T(8,128)} copy(f32[2048,8,128]{2,1,0:T(8,128)} %bitcast.147) | data formatting | bytes 16777216 | tf_op jit(solution)/shard_map/reshape | solution.py:103
  498.2 10.8 %fusion.9 = bf16[2048,8,128]{0,2,1:T(8,128)(2,1)} fusion(f32[2048,8,128]{0,2,1:T(8,128)} %copy.181, f32[8,128,128]{2,1,0:T(8,128)S(1)} %get-tuple-element.364, bf16[2048,8,128]{0,2,1:T(8,128)(2,1)} %bitcast.150, f32[2048]{0:T(1024)S(1)} %get-tuple-element.507), kind=kOutput, calls=%fused_computation.23 | convolution fusion | flops 3227516928 | bytes 17309696 | tf_op jit(solution)/shard_map/thf,hef->the/dot_general | solution.py:141
  515.5 11.9 %fusion.35 = f32[4,8,512,128]{3,2,1,0:T(8,128)} fusion(bf16[4,8,512,512]{3,2,1,0:T(8,128)(2,1)} %multiply_convert_fusion.1, bf16[4,512,8,128]{1,3,2,0:T(8,128)(2,1)} %copy.184), kind=kOutput, calls=%fused_computation.63 | convolution fusion | flops 2147483648 | bytes 29360128 | tf_op jit(solution)/shard_map/nhts,nthe->nshe/dot_general | solution.py:60
  527.3 8.2 %bitcast_add_fusion.8 = f32[4,512,8,128]{3,1,2,0:T(8,128)S(1)} fusion(f32[4,8,512,128]{3,2,1,0:T(8,128)} %fusion.35, f32[4,512]{1,0:T(4,128)S(1)} %copy-done.6, f32[4,8,128,128]{3,2,1,0:T(8,128)S(1)} %get-tuple-element.365, bf16[4,512,8,128]{3,2,1,0:T(8,128)(2,1)} %bitcast.140), kind=kOutput, calls=%fused_computation.21 | convolution fusion | flops 3225419776 | bytes 23076864 | tf_op jit(solution)/shard_map/nshf,nhef->nshe/dot_general | solution.py:94
  535.5 8.1 %copy.188 = f32[4,512,8,128]{3,2,1,0:T(8,128)} copy(f32[4,512,8,128]{3,1,2,0:T(8,128)S(1)} %bitcast_add_fusion.8) | data formatting | bytes 16777216 | tf_op jit(solution)/shard_map/add | solution.py:94
  543.6 9.4 %copy.190 = f32[2048,8,128]{0,2,1:T(8,128)} copy(f32[2048,8,128]{2,1,0:T(8,128)} %bitcast.148) | data formatting | bytes 16777216 | tf_op jit(solution)/shard_map/reshape | solution.py:104
  553.1 7.7 %fusion.36 = f32[4,8,128,512]{2,3,1,0:T(8,128)} fusion(f32[4,8,128,128]{3,2,1,0:T(8,128)S(1)} %get-tuple-element.365, bf16[4,512,8,128]{1,3,2,0:T(8,128)(2,1)} %copy.175), kind=kOutput, calls=%fused_computation.64 | convolution fusion | flops 3221225472 | bytes 14680064 | tf_op jit(solution)/shard_map/nshe,nhef->nshf/dot_general | solution.py:97
  560.7 17.0 %add_bitcast_fusion = f32[4,512,8,128]{3,1,2,0:T(8,128)} fusion(f32[4,8,128,512]{2,3,1,0:T(8,128)} %fusion.36, f32[4,512]{1,0:T(4,128)S(1)} %copy-done.6, bf16[4,8,512,512]{3,2,1,0:T(8,128)(2,1)} %multiply_convert_fusion, bf16[4,512,8,128]{1,0,3,2:T(4,128)(2,1)} %reshape_reshape.3), kind=kOutput, calls=%fused_computation.25 | convolution fusion | flops 2151677952 | bytes 37756928 | tf_op jit(solution)/shard_map/nhts,nthe->nshe/dot_general | solution.py:63
  577.7 11.7 %copy.198 = f32[4,512,8,128]{3,2,1,0:T(8,128)} copy(f32[4,512,8,128]{3,1,2,0:T(8,128)} %add_bitcast_fusion) | data formatting | bytes 16777216 | tf_op jit(solution)/shard_map/add | solution.py:97
  589.4 9.4 %copy.201 = f32[2048,8,128]{0,2,1:T(8,128)} copy(f32[2048,8,128]{2,1,0:T(8,128)} %bitcast.149) | data formatting | bytes 16777216 | tf_op jit(solution)/shard_map/reshape | solution.py:105
  598.9 11.1 %while.63 = (s32[]{:T(128)}, f32[8,128,128]{2,1,0:T(8,128)S(1)}, s32[]{:T(128)}, f32[4,8,128,128]{3,2,1,0:T(8,128)}, f32[4]{0:T(128)S(1)}, /*index=5*/s32[]{:T(128)}, s32[]{:T(128)}, s32[]{:T(128)}, s32[]{:T(128)}, f32[1]{0:T(128)}) while((s32[]{:T(128)}, f32[8,128,128]{2,1,0:T(8,128)S(1)}, s32[]{:T(128)}, ...), condition=%wide.region_9.10_spmd.clone, body=%wide.region_8.9_spmd.clone.sunk | while | flops 524297 | bytes 1573071 | solution.py:26
  610.0 10.9 %fusion.8 = bf16[2048,8,128]{0,2,1:T(8,128)(2,1)} fusion(f32[2048,8,128]{0,2,1:T(8,128)} %copy.190, f32[8,128,128]{2,1,0:T(8,128)S(1)} %get-tuple-element.367, bf16[2048,8,128]{2,1,0:T(8,128)(2,1)} %bitcast.141, f32[2048]{0:T(1024)S(1)} %copy-done.7), kind=kOutput, calls=%fused_computation.20 | convolution fusion | flops 3227516928 | bytes 17309696 | tf_op jit(solution)/shard_map/thf,hef->the/dot_general | solution.py:144
  627.5 11.7 %fusion.7 = bf16[2048,8,128]{0,2,1:T(8,128)(2,1)} fusion(f32[2048,8,128]{0,2,1:T(8,128)} %copy.201, f32[8,128,128]{2,1,0:T(8,128)S(1)} %get-tuple-element.367, bf16[2048,8,128]{2,1,0:T(8,128)(2,1)} %bitcast.143, f32[2048]{0:T(1024)S(1)} %copy-done.7), kind=kOutput, calls=%fused_computation.18 | convolution fusion | flops 3227516928 | bytes 17309696 | tf_op jit(solution)/shard_map/the,hef->thf/dot_general | solution.py:147
  645.6 56.1 %all-reduce.3.cloned.1.call-done = f32[1024,4096]{1,0:T(8,128)} async-done(((f32[1024,4096]{1,0:T(8,128)}), f32[1024,4096]{1,0:T(8,128)}) %all-reduce.3.cloned.1.call-update) | async-done | bytes 16777232 | tf_op jit(solution)/shard_map/psum | solution.py:158
  (108 shorter events, 113.8 us)
Async XLA Ops:
  7.2 124.7 %all-gather.8.cloned.1.call-start = ((), (), s32[]{:S(2)}) async-start(), calls=%async_computation.2 | async-start | bytes 2621440 | tf_op jit(solution)/shard_map/all_gather | solution.py:13
  8.4 5.4 copy-start.5
  16.9 7.6 %copy-start.8 = (s32[1,7]{1,0:T(1,128)S(1)}, s32[1,7]{1,0:T(1,128)}, u32[]{:S(2)}) copy-start(s32[1,7]{1,0:T(1,128)} %param.19) | copy-start | bytes 88
  43.1 0.8 copy-start.1
  43.1 16.7 %copy-start.3 = (f32[4,8,128,128]{3,2,1,0:T(8,128)}, f32[4,8,128,128]{3,2,1,0:T(8,128)S(1)}, u32[]{:S(2)}) copy-start(f32[4,8,128,128]{3,2,1,0:T(8,128)S(1)} %get-tuple-element.362) | copy-start | bytes 6291460
  43.1 3.7 copy-start.11
  43.9 326.4 %all-gather.6.cloned.1.call-start = ((), (), s32[]{:S(2)}) async-start(), calls=%async_computation | async-start | bytes 20971520 | tf_op jit(solution)/shard_map/all_gather | solution.py:121
  44.6 554.2 %all-gather.10.cloned.1.call-start = ((), (), s32[]{:S(2)}) async-start(), calls=%async_computation.3 | async-start | bytes 2621440 | tf_op jit(solution)/shard_map/all_gather | solution.py:13
  86.8 17.2 %copy-start.4 = (f32[4,8,128,128]{3,2,1,0:T(8,128)S(1)}, f32[4,8,128,128]{3,2,1,0:T(8,128)}, u32[]{:S(2)}) copy-start(f32[4,8,128,128]{3,2,1,0:T(8,128)} %copy-done.3) | copy-start | bytes 6291460
  142.8 10.8 %copy-start.9 = (f32[4]{0:T(128)}, f32[4]{0:T(128)S(1)}, u32[]{:S(2)}) copy-start(f32[4]{0:T(128)S(1)} %get-tuple-element.750) | copy-start | bytes 52
  445.9 0.8 copy-start
  446.7 255.0 %all-reduce.3.cloned.1.call-start = ((), (), s32[]{:S(2)}) async-start(), calls=%async_computation.1 | async-start | bytes 33554432 | tf_op jit(solution)/shard_map/psum | solution.py:158
  515.5 11.9 %copy-start.6 = (f32[4,512]{1,0:T(4,128)S(1)}, f32[4,512]{1,0:T(4,128)}, u32[]{:S(2)}) copy-start(f32[4,512]{1,0:T(4,128)} %get-tuple-element.502) | copy-start | bytes 24580
  589.4 9.5 %copy-start.2 = (f32[8,128,128]{2,1,0:T(8,128)S(1)}, f32[8,128,128]{2,1,0:T(8,128)}, u32[]{:S(2)}) copy-start(f32[8,128,128]{2,1,0:T(8,128)} %custom-call.3) | copy-start | bytes 1572868
  589.4 9.5 %copy-start.10 = (f32[4]{0:T(128)S(1)}, f32[4]{0:T(128)}, u32[]{:S(2)}) copy-start(f32[4]{0:T(128)} %copy-done.9) | copy-start | bytes 52
  598.9 11.1 %copy-start.7 = (f32[2048]{0:T(1024)S(1)}, f32[2048]{0:T(1024)}, u32[]{:S(2)}) copy-start(f32[2048]{0:T(1024)} %get-tuple-element.506) | copy-start | bytes 24580
Sparse Core Ops, SparseCore 0:
  44.0 37.8 all-gather.7
  83.5 286.7 all-gather.5
  446.8 33.3 all-gather.9
  483.9 217.7 all-reduce.2
where the time goes:
time: 718 us; the launch traced here: 712 us
  waiting for transfers between devices  273 us (38%)
  matrix products  223 us (31%)
  local copies, waits for them, and re-layouts  147 us (20%)
  other arithmetic  34.7 us (5%)
  between operations  15.6 us (2%)
  blocking collectives  11.7 us (2%)
    all_gather x1, waiting for transfers between devices, on_device(): lax.all_gather(out_cotangent, 'head', axis=2, tiled=True)[0]  217 us
    psum x1, waiting for transfers between devices, on_device(): summed = lax.psum(partial_grad, ('seq', 'rep'))  56.1 us
    unnamed x33, local copies, waits for them, and re-layouts  36.1 us
    dot_general x1, matrix products, on_device(): lax.dot_general(full_cotangent, out_weight, (((1,), (1,)), ((), ())), pre...  24.1 us
    dot_general x1, matrix products, on_device(): lax.dot_general(attention_out, full_cotangent, (((0,), (0,)), ((), ())),...  23.6 us
    dot_general x1, matrix products, local_pass(): jnp.einsum('nhts,nshe->nthe', attn, value_blocks, preferred_element_type=...  17.2 us
    dot_general x1, matrix products, local_pass(): jnp.einsum('nhts,nthe->nshe', attn, grad_blocks, preferred_element_type=j...  17 us
    add x8, other arithmetic, link_step(): return (item[0] + item[1] * state, state)  15 us
  transfers between devices with their start and end apart: 4, of which 2 were waited for; matrix products, arithmetic and copies ran while one was open for 41% of the time, Pallas kernels for 0%

commit v1 on v0

--- a/solution.py
+++ b/solution.py
@@ -2,10 +2,19 @@
 import jax.numpy as jnp
 from jax import lax
 from jax.sharding import PartitionSpec as P
+from jax.lax import all_to_all, psum
 
 HD = 128
 BLOCK = 512
 highest = lax.Precision.HIGHEST
+
+
+def _build_tiles(body):
+    dev_n = psum(1, "head")
+    all_blocks = tuple((dev_n if d == 2 else 1 for d in range(body.ndim)))
+    f_now = jnp.tile(body, all_blocks)
+    formed = all_to_all(f_now, "head", split_axis=2, concat_axis=2, tiled=True)
+    return formed
 
 
 def prefix(shard, axis, combine, identity, reverse):
@@ -118,7 +127,7 @@
     queries = query_heads[0].reshape(length, heads, HD)
     keys = key_heads[0].reshape(length, heads, HD)
     values = value_heads[0].reshape(length, heads, HD)
-    full_cotangent = lax.all_gather(out_cotangent, "head", axis=2, tiled=True)[0]
+    full_cotangent = _build_tiles(out_cotangent)[0]
     grads_flat = lax.dot_general(
         full_cotangent, out_weight, (((1,), (1,)), ((), ())), preferred_element_type=jnp.float32
     ).astype(jnp.bfloat16)

time: 718 us -> 977 us (1.36)
  local copies, waits for them, and re-layouts: 147 us -> 312 us
  other arithmetic: 34.7 us -> 132 us
  waiting for transfers between devices: 273 us -> 259 us
    all_to_all x0 -> x1, waiting for transfers between devices: none -> 221 us  [_build_tiles(): formed = all_to_all(f_now, 'head', split_axis=2, concat_axis=2, tiled=True)]
    all_gather x1 -> x0, waiting for transfers between devices: 217 us -> none  [on_device(): lax.all_gather(out_cotangent, 'head', axis=2, tiled=True)[0]]
    unnamed x4 -> x5, other arithmetic: 0.01 us -> 99.6 us
    all_to_all x0 -> x1, local copies, waits for them, and re-layouts: none -> 70.4 us  [_build_tiles(): formed = all_to_all(f_now, 'head', split_axis=2, concat_axis=2, tiled=True)]
    unnamed x33 -> x44, local copies, waits for them, and re-layouts: 36.1 us -> 90.7 us
    another operation x2 -> x5, local copies, waits for them, and re-layouts: 0.45 us -> 40.9 us  [the longest x3 40.5 us: _build_tiles(): f_now = jnp.tile(body, all_blocks)]
    psum x1, waiting for transfers between devices: 56.1 us -> 38.3 us  [on_device(): summed = lax.psum(partial_grad, ('seq', 'rep'))]
  transfers between devices with their start and end apart: 4 -> 4, of which waited for: 2 -> 2; matrix products, arithmetic and copies ran while one was open for 41% -> 35% of each run, Pallas kernels for 0% -> 0%
where the time goes in v1:
time: 977 us; the launch traced here: 966 us
  local copies, waits for them, and re-layouts  312 us (32%)
  waiting for transfers between devices  259 us (27%)
  matrix products  221 us (23%)
  other arithmetic  132 us (14%)
  between operations  15.5 us (2%)
  blocking collectives  11.6 us (1%)
    all_to_all x1, waiting for transfers between devices, _build_tiles(): formed = all_to_all(f_now, 'head', split_axis=2, concat_axis=2, tiled=True)  221 us
    unnamed x5, other arithmetic  99.6 us
    unnamed x44, local copies, waits for them, and re-layouts  90.7 us
    all_to_all x1, local copies, waits for them, and re-layouts, _build_tiles(): formed = all_to_all(f_now, 'head', split_axis=2, concat_axis=2, tiled=True)  70.4 us
    another operation x3, local copies, waits for them, and re-layouts, _build_tiles(): f_now = jnp.tile(body, all_blocks)  40.5 us
    psum x1, waiting for transfers between devices, on_device(): summed = lax.psum(partial_grad, ('seq', 'rep'))  38.3 us
    dot_general x1, matrix products, on_device(): lax.dot_general(full_cotangent, out_weight, (((1,), (1,)), ((), ())), pre...  24.1 us
    dot_general x1, matrix products, on_device(): lax.dot_general(attention_out, full_cotangent, (((0,), (0,)), ((), ())),...  23.4 us
  transfers between devices with their start and end apart: 4, of which 2 were waited for; matrix products, arithmetic and copies ran while one was open for 35% of the time, Pallas kernels for 0%

profile of v1, /device:TPU:0, one launch (start us, length us, event | category | flops | bytes accessed | tf_op | source)
XLA Modules:
  0.0 965.6 jit_solution(17694565220611697482)
XLA Ops:
  17.9 29.8 %copy.301 = bf16[1,2048,4096]{1,0,2:T(2,128)(2,1)} copy(bf16[1,2048,4096]{1,2,0:T(8,128)(2,1)S(1)} %bitcast.150) | data formatting | bytes 33554432 | tf_op jit(solution)/shard_map/tile | solution.py:15
  48.1 99.6 %reduce.5 = bf16[4096,2048]{1,0:T(8,128)(2,1)} reduce(bf16[4096,1,2048]{2,1,0:T(2,128)(2,1)} %bitcast.143, bf16[]{:T(256)} %broadcast.123), dimensions={1}, to_apply=%bitcast.122.reduce_sub_computation | reduce | bytes 33554432
  147.8 17.0 %reshape.206 = bf16[4,2,1048576]{2,1,0:T(2,128)(2,1)} reshape(bf16[4096,2048]{1,0:T(8,128)(2,1)} %reduce.5) | data formatting | bytes 33554432
  198.9 10.0 %while.60 = (s32[]{:T(128)}, f32[8,128,128]{2,1,0:T(8,128)S(1)}, f32[4,8,128,128]{3,2,1,0:T(8,128)S(1)}, f32[4,8,128,128]{3,2,1,0:T(8,128)}, f32[4]{0:T(128)S(1)}, /*index=5*/s32[]{:T(128)}, s32[]{:T(128)}) while((s32[]{:T(128)}, f32[8,128,128]{2,1,0:T(8,128)S(1)}, f32[4,8,128,128]{3,2,1,0:T(8,128)S(1)}, ...), condition=%wide.region_3.4_spmd.clone, body=%wide.region_2.3_spmd.clone.sunk | while | flops 524291 | bytes 2621552 | solution.py:93
  228.4 11.5 %multiply_convert_fusion = bf16[4,8,512,512]{3,2,1,0:T(8,128)(2,1)} fusion(f32[4,512,512]{2,1,0:T(8,128)} %and_convert_fusion, bf16[4,512,8,128]{1,3,2,0:T(8,128)(2,1)} %copy.232, bf16[4,512,8,128]{1,3,2,0:T(8,128)(2,1)} %copy.223), kind=kOutput, calls=%fused_computation.8 | convolution fusion | flops 2164260864 | bytes 29360128 | tf_op jit(solution)/shard_map/nthe,nshe->nhts/dot_general | solution.py:57
  239.9 11.6 %all-reduce = f32[4]{0:T(128)S(1)} all-reduce(f32[4]{0:T(128)S(1)} %dynamic-update-slice), channel_id=1, replica_groups=mesh['seq'=4,'head'=4,'rep'=2] {'seq'}, use_global_device_ids=true, to_apply=%add | all-reduce | flops 4 | bytes 32
  251.5 14.7 %fusion.24 = f32[4,8,512,128]{3,2,1,0:T(8,128)} fusion(bf16[4,8,512,512]{3,2,1,0:T(8,128)(2,1)} %multiply_convert_fusion, bf16[4,512,8,128]{3,2,1,0:T(8,128)(2,1)} %bitcast.146), kind=kOutput, calls=%fused_computation.39 | convolution fusion | flops 2147483648 | bytes 29360128 | tf_op jit(solution)/shard_map/nhts,nshe->nthe/dot_general | solution.py:65
  266.2 8.2 bitcast_add_fusion.5
  282.5 9.3 copy.257
  293.6 11.2 %while.61 = (s32[]{:T(128)}, f32[8,128,128]{2,1,0:T(8,128)S(1)}, s32[]{:T(128)}, f32[4,8,128,128]{3,2,1,0:T(8,128)}, f32[4]{0:T(128)S(1)}, /*index=5*/s32[]{:T(128)}, f32[1]{0:T(128)}, s32[]{:T(128)}) while((s32[]{:T(128)}, f32[8,128,128]{2,1,0:T(8,128)S(1)}, s32[]{:T(128)}, f32[4,8,128,128]{3,2,1,0:T(8,128)}, f32[4]{0:T(128)S(1)}, ...), condition=%wide.region_5.6_spmd.clone, body=%wide.region_4.5_spmd.clone.sunk | while | flops 524293 | bytes 1573001 | solution.py:35
  304.8 10.9 %fusion.6 = bf16[2048,8,128]{0,2,1:T(8,128)(2,1)} fusion(f32[2048,8,128]{0,2,1:T(8,128)} %copy.257, f32[8,128,128]{2,1,0:T(8,128)S(1)} %get-tuple-element.364, bf16[2048,8,128]{2,1,0:T(8,128)(2,1)} %bitcast.154, f32[2048]{0:T(1024)S(1)} %get-tuple-element.511), kind=kOutput, calls=%fused_computation.15 | convolution fusion | flops 3227516928 | bytes 17309696 | tf_op jit(solution)/shard_map/the,hef->thf/dot_general | solution.py:147
  315.7 220.7 %all-to-all-done = bf16[4,2,1048576]{2,1,0:T(2,128)(2,1)} async-done(((bf16[4,2,1048576]{2,1,0:T(2,128)(2,1)}), bf16[4,2,1048576]{2,1,0:T(2,128)(2,1)}, u32[]{:S(2)}, u32[]{:S(2)}) %all-to-all-start) | async-done | bytes 16777248 | tf_op jit(solution)/shard_map/all_to_all | solution.py:16
  536.5 35.7 %reshape.207 = bf16[4096,1,2048]{2,1,0:T(2,128)(2,1)} reshape(bf16[4,2,1048576]{2,1,0:T(2,128)(2,1)} %all-to-all-done) | data formatting | bytes 33554432
  572.1 70.4 %copy.219 = bf16[1,2048,4096]{2,1,0:T(8,128)(2,1)} copy(bf16[1,2048,4096]{1,0,2:T(2,128)(2,1)} %bitcast.144) | data formatting | bytes 33554432 | tf_op jit(solution)/shard_map/all_to_all | solution.py:16
  642.5 24.1 %fusion.17 = bf16[2048,1024]{0,1:T(8,128)(2,1)} fusion(bf16[1024,4096]{1,0:T(8,128)(2,1)} %param.18, bf16[1,2048,4096]{2,1,0:T(8,128)(2,1)} %copy.219), kind=kOutput, calls=%fused_computation.34 | convolution fusion | flops 17181966336 | bytes 29360128 | tf_op jit(solution)/shard_map/dot_general | solution.py:131
  681.2 10.0 %while.62 = (s32[]{:T(128)}, f32[8,128,128]{2,1,0:T(8,128)S(1)}, f32[4,8,128,128]{3,2,1,0:T(8,128)S(1)}, f32[4,8,128,128]{3,2,1,0:T(8,128)}, f32[4]{0:T(128)S(1)}, /*index=5*/s32[]{:T(128)}, s32[]{:T(128)}, s32[]{:T(128)}) while((s32[]{:T(128)}, f32[8,128,128]{2,1,0:T(8,128)S(1)}, f32[4,8,128,128]{3,2,1,0:T(8,128)S(1)}, ...), condition=%wide.region_7.8_spmd.clone, body=%wide.region_6.7_spmd.clone.sunk | while | flops 524292 | bytes 2621572 | solution.py:94
  699.2 16.5 %add_bitcast_fusion = f32[4,512,8,128]{3,1,2,0:T(8,128)} fusion(f32[4,8,128,512]{2,3,1,0:T(8,128)} %fusion.36, f32[4,512]{1,0:T(4,128)S(1)} %get-tuple-element.506, bf16[4,8,512,512]{3,2,1,0:T(8,128)(2,1)} %multiply_convert_fusion, bf16[4,512,8,128]{1,0,3,2:T(4,128)(2,1)} %reshape_reshape.3), kind=kOutput, calls=%fused_computation.25 | convolution fusion | flops 2151677952 | bytes 37756928 | tf_op jit(solution)/shard_map/nhts,nthe->nshe/dot_general | solution.py:72
  715.7 23.4 %fusion.2 = f32[1024,4096]{1,0:T(8,128)} fusion(bf16[2048,1024]{0,1:T(8,128)(2,1)} %bitcast.167, bf16[1,2048,4096]{2,1,0:T(8,128)(2,1)} %copy.219), kind=kOutput, calls=%fused_computation.10 | convolution fusion | flops 17179869184 | bytes 37748736 | tf_op jit(solution)/shard_map/dot_general | solution.py:164
  739.1 12.0 %multiply_convert_fusion.1 = bf16[4,8,512,512]{3,2,1,0:T(8,128)(2,1)} fusion(f32[4,512,512]{2,1,0:T(8,128)} %and_convert_fusion, bf16[4,512,8,128]{1,0,3,2:T(4,128)(2,1)} %reshape_reshape.3, bf16[4,512,8,128]{3,2,1,0:T(8,128)(2,1)} %bitcast.147), kind=kOutput, calls=%fused_computation.9 | convolution fusion | flops 2164260864 | bytes 29360128 | tf_op jit(solution)/shard_map/nthe,nshe->nhts/dot_general | solution.py:61
  751.1 11.6 %copy.246 = f32[4,512,8,128]{3,2,1,0:T(8,128)} copy(f32[4,512,8,128]{3,1,2,0:T(8,128)} %add_bitcast_fusion) | data formatting | bytes 16777216 | tf_op jit(solution)/shard_map/add | solution.py:106
  762.7 9.6 copy.249
  772.4 11.7 %fusion.35 = f32[4,8,512,128]{3,2,1,0:T(8,128)} fusion(bf16[4,8,512,512]{3,2,1,0:T(8,128)(2,1)} %multiply_convert_fusion.1, bf16[4,512,8,128]{1,3,2,0:T(8,128)(2,1)} %copy.232), kind=kOutput, calls=%fused_computation.64 | convolution fusion | flops 2147483648 | bytes 29360128 | tf_op jit(solution)/shard_map/nhts,nthe->nshe/dot_general | solution.py:69
  784.1 8.1 bitcast_add_fusion.8
  800.2 9.4 copy.238
  809.7 15.2 %fusion.34 = f32[4,8,512,128]{3,2,1,0:T(8,128)} fusion(bf16[4,8,512,512]{3,2,1,0:T(8,128)(2,1)} %multiply_convert_fusion.1, bf16[4,512,8,128]{1,3,2,0:T(8,128)(2,1)} %copy.223), kind=kOutput, calls=%fused_computation.63 | convolution fusion | flops 2147483648 | bytes 29360128 | tf_op jit(solution)/shard_map/nhts,nshe->nthe/dot_general | solution.py:68
  824.9 10.5 %bitcast_add_fusion.10 = f32[4,512,8,128]{3,1,2,0:T(8,128)S(1)} fusion(f32[4,8,512,128]{3,2,1,0:T(8,128)} %fusion.34, f32[4,512]{1,0:T(4,128)S(1)} %copy-done.8, f32[4,8,128,128]{3,2,1,0:T(8,128)S(1)} %copy-done.6, bf16[4,512,8,128]{1,0,3,2:T(4,128)(2,1)} %reshape_reshape.3), kind=kOutput, calls=%fused_computation.24 | convolution fusion | flops 3225419776 | bytes 23076864 | tf_op jit(solution)/shard_map/nthf,nhef->nthe/dot_general | solution.py:100
  843.5 9.6 copy.229
  853.1 11.1 %fusion.9 = bf16[2048,8,128]{0,2,1:T(8,128)(2,1)} fusion(f32[2048,8,128]{0,2,1:T(8,128)} %copy.229, f32[8,128,128]{2,1,0:T(8,128)S(1)} %copy-done.4, bf16[2048,8,128]{0,2,1:T(8,128)(2,1)} %bitcast.159, f32[2048]{0:T(1024)S(1)} %copy-done.11), kind=kOutput, calls=%fused_computation.23 | convolution fusion | flops 3227516928 | bytes 17309696 | tf_op jit(solution)/shard_map/thf,hef->the/dot_general | solution.py:150
  870.7 11.0 %while.63 = (s32[]{:T(128)}, f32[8,128,128]{2,1,0:T(8,128)S(1)}, s32[]{:T(128)}, f32[4,8,128,128]{3,2,1,0:T(8,128)}, f32[4]{0:T(128)S(1)}, /*index=5*/s32[]{:T(128)}, s32[]{:T(128)}, s32[]{:T(128)}, s32[]{:T(128)}, f32[1]{0:T(128)}) while((s32[]{:T(128)}, f32[8,128,128]{2,1,0:T(8,128)S(1)}, s32[]{:T(128)}, ...), condition=%wide.region_9.10_spmd.clone, body=%wide.region_8.9_spmd.clone.sunk | while | flops 524297 | bytes 1573063 | solution.py:35
  881.8 11.8 %fusion.7 = bf16[2048,8,128]{0,2,1:T(8,128)(2,1)} fusion(f32[2048,8,128]{0,2,1:T(8,128)} %copy.249, f32[8,128,128]{2,1,0:T(8,128)S(1)} %get-tuple-element.367, bf16[2048,8,128]{2,1,0:T(8,128)(2,1)} %bitcast.152, f32[2048]{0:T(1024)S(1)} %copy-done.9), kind=kOutput, calls=%fused_computation.18 | convolution fusion | flops 3227516928 | bytes 17309696 | tf_op jit(solution)/shard_map/the,hef->thf/dot_general | solution.py:156
  900.2 10.8 %fusion.8 = bf16[2048,8,128]{0,2,1:T(8,128)(2,1)} fusion(f32[2048,8,128]{0,2,1:T(8,128)} %copy.238, f32[8,128,128]{2,1,0:T(8,128)S(1)} %get-tuple-element.367, bf16[2048,8,128]{2,1,0:T(8,128)(2,1)} %bitcast.149, f32[2048]{0:T(1024)S(1)} %copy-done.9), kind=kOutput, calls=%fused_computation.20 | convolution fusion | flops 3227516928 | bytes 17309696 | tf_op jit(solution)/shard_map/thf,hef->the/dot_general | solution.py:153
  917.4 38.3 %all-reduce.3.cloned.1.call-done = f32[1024,4096]{1,0:T(8,128)} async-done(((f32[1024,4096]{1,0:T(8,128)}), f32[1024,4096]{1,0:T(8,128)}) %all-reduce.3.cloned.1.call-update) | async-done | bytes 16777232 | tf_op jit(solution)/shard_map/psum | solution.py:167
  (123 shorter events, 171.0 us)
Async XLA Ops:
  164.8 7.8 copy-start.12
  164.8 371.7 %all-to-all-start = ((bf16[4,2,1048576]{2,1,0:T(2,128)(2,1)}), bf16[4,2,1048576]{2,1,0:T(2,128)(2,1)}, u32[]{:S(2)}, u32[]{:S(2)}) async-start(bf16[4,2,1048576]{2,1,0:T(2,128)(2,1)} %reshape.206), calls=%async_computation | async-start | bytes 33554432 | tf_op jit(solution)/shard_map/all_to_all | solution.py:16
  172.0 121.6 %all-gather.5.cloned.1.call-start = ((), (), s32[]{:S(2)}) async-start(), calls=%async_computation.2 | async-start | bytes 2621440 | tf_op jit(solution)/shard_map/all_gather | solution.py:22
  209.0 0.8 copy-start.1
  209.0 57.2 %copy-start.5 = (f32[4,8,128,128]{3,2,1,0:T(8,128)}, f32[4,8,128,128]{3,2,1,0:T(8,128)S(1)}, u32[]{:S(2)}) copy-start(f32[4,8,128,128]{3,2,1,0:T(8,128)S(1)} %get-tuple-element.362) | copy-start | bytes 6291460
  209.8 660.9 %all-gather.7.cloned.1.call-start = ((), (), s32[]{:S(2)}) async-start(), calls=%async_computation.3 | async-start | bytes 2621440 | tf_op jit(solution)/shard_map/all_gather | solution.py:22
  215.8 8.8 copy-start.15
  251.5 14.7 %copy-start.7 = (f32[4,512]{1,0:T(4,128)}, f32[4,512]{1,0:T(4,128)S(1)}, u32[]{:S(2)}) copy-start(f32[4,512]{1,0:T(4,128)S(1)} %convert_element_type.133) | copy-start | bytes 24580
  293.6 22.1 %copy-start.10 = (f32[2048]{0:T(1024)}, f32[2048]{0:T(1024)S(1)}, u32[]{:S(2)}) copy-start(f32[2048]{0:T(1024)S(1)} %get-tuple-element.511) | copy-start | bytes 24580
  304.8 10.9 %copy-start.3 = (f32[8,128,128]{2,1,0:T(8,128)}, f32[8,128,128]{2,1,0:T(8,128)S(1)}, u32[]{:S(2)}) copy-start(f32[8,128,128]{2,1,0:T(8,128)S(1)} %get-tuple-element.364) | copy-start | bytes 1572868
  304.8 10.9 %copy-start.13 = (f32[4]{0:T(128)}, f32[4]{0:T(128)S(1)}, u32[]{:S(2)}) copy-start(f32[4]{0:T(128)S(1)} %get-tuple-element.752) | copy-start | bytes 52
  691.2 7.9 copy-start
  699.1 256.6 %all-reduce.3.cloned.1.call-start = ((), (), s32[]{:S(2)}) async-start(), calls=%async_computation.1 | async-start | bytes 33554432 | tf_op jit(solution)/shard_map/psum | solution.py:167
  809.7 15.2 %copy-start.6 = (f32[4,8,128,128]{3,2,1,0:T(8,128)S(1)}, f32[4,8,128,128]{3,2,1,0:T(8,128)}, u32[]{:S(2)}) copy-start(f32[4,8,128,128]{3,2,1,0:T(8,128)} %copy-done.5) | copy-start | bytes 6291460
  809.7 15.2 %copy-start.8 = (f32[4,512]{1,0:T(4,128)S(1)}, f32[4,512]{1,0:T(4,128)}, u32[]{:S(2)}) copy-start(f32[4,512]{1,0:T(4,128)} %copy-done.7) | copy-start | bytes 24580
  843.5 9.6 copy-start.4
  843.5 9.7 copy-start.11
  864.2 6.5 copy-start.2
  864.2 6.5 copy-start.14
  870.7 11.0 %copy-start.9 = (f32[2048]{0:T(1024)S(1)}, f32[2048]{0:T(1024)}, u32[]{:S(2)}) copy-start(f32[2048]{0:T(1024)} %get-tuple-element.510) | copy-start | bytes 24580
Sparse Core Ops, SparseCore 0:
  209.9 38.1 all-gather.4
  699.3 34.4 all-gather.6
  739.3 216.4 all-reduce.2
